TPU v7x, 32 devices: a whole 2x2x4 slice. The times are simulated.
32 devices in a mesh: sector: 8 (over y, x, core), slab: 4 (over z).
Axes of the slice: x: 2, y: 2, z: 4, core: 2. Of those that a mesh axis runs over, the one named last changes fastest.
Arguments:
- iterate: float32 [32, 60, 4096], P('slab', None, 'sector'), may hold values from -6 to 6
- right_side: float32 [32, 60, 4096], P('slab', None, 'sector'), may hold values from -6 to 6
- geometry: float32 [32, 3, 4096], P('slab', None, 'sector'), may hold values from 0.5 to 2
- temporal_block_scale: float32 [32, 4096], P('slab', 'sector'), may hold values from 1 to 2.1
- decay_rates: float32 [60], replicated, may hold values from 0.49 to 0.996
- neighbour_index: int32 [5, 4096], P(None, 'sector'), may hold values from 0 to 511, as said below
- neighbour_side: int32 [5, 4096], P(None, 'sector'), may hold values from -1 to 1, as said below
- orientation: int32 [5, 4096], P(None, 'sector'), may hold values from 0 to 2
- sector_counts: int32 [8], P('sector'), may hold values from 384 to 512, as said below
- volume_ops: float32 [4, 60, 60], replicated, may hold values from -0.75 to 0.75
- face_ops: float32 [5, 60, 180], replicated, may hold values from -0.75 to 0.75
- time_coupling: float32 [60, 60], replicated, may hold values from -0.75 to 0.75
- precondition: float32 [60, 60], replicated, may hold values from -0.375 to 0.375
Outputs:
- smoothed: float32 [32, 60, 4096], P('slab', None, 'sector')
- final_section_residual: float32 [32, 60, 4096], P('slab', None, 'sector')
Inputs may be any that keep to these rules, and one draw needn't show every extreme that they name: `sector_counts`: each sector holds from 384 to 512 live elements; some sector is full and some holds exactly 384. `neighbour_index`: faces of live elements name live elements; the first face of a slot below 192 names a slot of 320 or more, of the preceding sector or of its own; the first face of a slot from 320 up names a slot below 192, of the following sector or of its own; all other faces stay in the sector. `neighbour_side`: only the first face of a slot below 192 or from 320 up may leave the sector.
All inputs are finite; a program needn't handle non-finite values.
Results may differ from a plain program's by a relative error of at most 0.0042.
Values may be sent and summed in bfloat16 or wider, within the bound.
A program may use at most 64 MiB of HBM per device.

v0:
```python
import jax
import jax.numpy as jnp
from jax import lax
from jax.sharding import PartitionSpec as P

SECTIONS = 2
RELAX = 0.8
HIGH = lax.Precision.HIGHEST


def shifted(block, axis, distance):
    devices = range(lax.axis_size(axis))
    route = [((i - distance) % len(devices), i) for i in devices]
    return lax.ppermute(block, axis, route)


def padded(cells, sides, width):
    for axis, dim in sides:
        count = lax.axis_size(axis)
        head = lax.slice_in_dim(cells, 0, width, axis=dim)
        tail = lax.slice_in_dim(cells, cells.shape[dim] - width, cells.shape[dim], axis=dim)
        cells = jnp.concatenate(
            [
                lax.ppermute(tail, axis, [(i, (i + 1) % count) for i in range(count)]),
                cells,
                lax.ppermute(head, axis, [((i + 1) % count, i) for i in range(count)]),
            ],
            axis=dim,
        )
    return cells


def entering_2(value, axis, join, neutral):
    count, mine = (lax.axis_size(axis), lax.axis_index(axis))
    pieces = lax.all_gather(value, axis)
    so_far = jnp.full_like(value, 0) + jnp.asarray(neutral, value.dtype)

    def hop(position, so_far):
        longer = join(so_far, pieces[position])
        return jnp.where(position < mine, longer, so_far)

    return lax.fori_loop(0, count - 1, hop, so_far)


def broadcast(value, axis, source):
    kept = jnp.where(lax.axis_index(axis) == source, value, 0).astype(value.dtype)
    return lax.psum(kept, axis)


def operate(field, geometry, place, masks, volume_ops, face_ops, time_coupling, width):
    last_slab = shifted(field[-1], "slab", 1)
    previous = jnp.concatenate([last_slab[None], field[:-1]], axis=0)
    terms = jnp.einsum("dij,sje->sdie", volume_ops, field, precision=HIGH)
    applied = terms[:, 0] + jnp.sum(geometry[:, :, None, :] * terms[:, 1:], axis=1)
    extended = padded(field, (("sector", 2),), width)
    for face_id in range(face_ops.shape[0]):
        picked = jnp.take(extended, place[face_id], axis=2)
        stacked = jnp.concatenate(
            [picked * masks[face_id, rotation][None, None, :] for rotation in range(3)], axis=1
        )
        applied = applied + jnp.einsum("ij,sje->sie", face_ops[face_id], stacked, precision=HIGH)
    return applied - jnp.einsum("ij,sje->sie", time_coupling, previous, precision=HIGH)


def multiply_join(earlier, later):
    return earlier * later


def adding_join(earlier, later):
    return earlier + later


def gain_setup(scale, rate):
    factor = rate[None] / scale[:, None, :]
    own_gain = jnp.prod(factor, axis=0)
    unity = jnp.ones_like(own_gain)
    before_gain = entering_2(own_gain, "slab", multiply_join, unity)
    through_gain = before_gain * own_gain
    total_gain = broadcast(through_gain, "slab", lax.axis_size("slab") - 1)
    return (factor, before_gain, through_gain, total_gain)


def periodic_scan(source, scale, gains):
    factor, before_gain, through_gain, total_gain = gains
    values = lax.optimization_barrier(source).astype(jnp.float32)
    offset = values / scale[:, None, :]

    def compose(state, items):
        step_gain, step_offset = items
        return (step_gain * state + step_offset, None)

    nothing = jnp.zeros_like(values[0])
    own_offset, _ = lax.scan(compose, nothing, (factor, offset))
    scaled = own_offset / through_gain
    earlier = entering_2(scaled, "slab", adding_join, nothing)
    everything = lax.psum(scaled, "slab")
    before_offset = before_gain * earlier
    total_offset = total_gain * everything
    closing = total_offset / (1.0 - total_gain)
    entering = before_gain * closing + before_offset

    def advance(state, items):
        step_gain, step_offset = items
        state = step_gain * state + step_offset
        return (state, state)

    _, solved = lax.scan(advance, entering, (factor, offset))
    return solved


def on_device(
    iterate,
    right_side,
    geometry,
    temporal_block_scale,
    decay_rates,
    neighbour_index,
    neighbour_side,
    orientation,
    sector_counts,
    volume_ops,
    face_ops,
    time_coupling,
    precondition,
):
    count = iterate.shape[2]
    width = 3 * count // 8
    slots = jnp.arange(count, dtype=jnp.int32)
    live = ((slots < sector_counts[0] - width) | (slots >= count - width)).astype(jnp.float32)
    place = jnp.where(
        neighbour_side == 0,
        width + neighbour_index,
        jnp.where(
            neighbour_side < 0, neighbour_index - (count - width), count + width + neighbour_index
        ),
    )
    masks = jnp.stack(
        [(orientation == rotation).astype(jnp.float32) for rotation in range(3)], axis=1
    )
    rate = decay_rates[:, None]
    gains = gain_setup(temporal_block_scale, rate)
    field = iterate
    residual = right_side
    for section_id in range(SECTIONS):
        applied = operate(field, geometry, place, masks, volume_ops, face_ops, time_coupling, width)
        residual = live[None, None, :] * (right_side - applied)
        source = jnp.einsum("ij,sje->sie", precondition, residual, precision=HIGH).astype(
            jnp.bfloat16
        )
        correction = periodic_scan(source, temporal_block_scale, gains).astype(jnp.bfloat16)
        field = field + RELAX * correction.astype(jnp.float32)
    return (field, residual)


def solution(mesh):
    in_specs = (
        P("slab", None, "sector"),
        P("slab", None, "sector"),
        P("slab", None, "sector"),
        P("slab", "sector"),
        P(),
        P(None, "sector"),
        P(None, "sector"),
        P(None, "sector"),
        P("sector"),
        P(),
        P(),
        P(),
        P(),
    )
    out_specs = (P("slab", None, "sector"), P("slab", None, "sector"))
    return jax.shard_map(
        on_device, mesh=mesh, in_specs=in_specs, out_specs=out_specs, check_vma=False
    )
```

profile of v0, /device:TPU:0, one launch (start us, length us, event | category | flops | bytes accessed | tf_op | source)
XLA Modules:
  0.0 390.7 jit_solution(17648043873069906003)
XLA Ops:
  22.6 5.2 %convolution_bitcast_fusion.1 = f32[8,4,60,512]{3,2,1,0:T(8,128)} fusion(f32[8,60,512,1]{2,0,1,3:T(8,128)S(1)} %bitcast.258, f32[4,60,60]{2,0,1:T(4,128)S(1)} %copy-done.34), kind=kOutput, calls=%fused_computation.88 | convolution fusion | flops 707788800 | bytes 4972800 | tf_op jit(solution)/shard_map/dij,sje->sdie/dot_general | solution.py:53
  29.2 3.5 fusion.1
  34.3 4.4 %copy.60 = f32[8,60,896]{1,0,2:T(8,128)} copy(f32[8,60,896]{2,0,1:T(8,128)} %pad_maximum_fusion.1) | data formatting | bytes 3440640 | tf_op jit(solution)/shard_map/concatenate | solution.py:22
  38.8 4.3 %gather_fusion = f32[512,8,60]{2,1,0:T(8,128)} fusion(f32[8,60,896]{1,0,2:T(8,128)} %copy.60, s32[1024]{0:T(1024)S(1)} %pad_clamp_fusion.4), kind=kCustom, calls=%fused_computation.clone | custom fusion | bytes 1968128 | tf_op jit(solution)/shard_map/jit(_take)/gather | solution.py:57
  43.1 3.2 copy.61
  46.3 4.3 %gather_fusion.1 = f32[512,8,60]{2,1,0:T(8,128)} fusion(f32[8,60,896]{1,0,2:T(8,128)} %copy.60, s32[1024]{0:T(1024)S(1)} %pad_clamp_fusion.3), kind=kCustom, calls=%fused_computation.1.clone | custom fusion | bytes 1968128 | tf_op jit(solution)/shard_map/jit(_take)/gather | solution.py:57
  50.6 3.2 copy.63
  53.9 4.3 %gather_fusion.2 = f32[512,8,60]{2,1,0:T(8,128)} fusion(f32[8,60,896]{1,0,2:T(8,128)} %copy.60, s32[1024]{0:T(1024)S(1)} %pad_clamp_fusion.2), kind=kCustom, calls=%fused_computation.2.clone | custom fusion | bytes 1968128 | tf_op jit(solution)/shard_map/jit(_take)/gather | solution.py:57
  58.2 3.2 copy.65
  61.4 4.3 %gather_fusion.3 = f32[512,8,60]{2,1,0:T(8,128)} fusion(f32[8,60,896]{1,0,2:T(8,128)} %copy.60, s32[1024]{0:T(1024)S(1)} %pad_clamp_fusion.1), kind=kCustom, calls=%fused_computation.3.clone | custom fusion | bytes 1968128 | tf_op jit(solution)/shard_map/jit(_take)/gather | solution.py:57
  67.9 4.3 %gather_fusion.4 = f32[512,8,60]{2,1,0:T(8,128)} fusion(f32[8,60,896]{1,0,2:T(8,128)} %copy.60, s32[1024]{0:T(1024)S(1)} %pad_clamp_fusion), kind=kCustom, calls=%fused_computation.4.clone | custom fusion | bytes 1968128 | tf_op jit(solution)/shard_map/jit(_take)/gather | solution.py:57
  76.3 4.6 %fusion.119 = f32[8,60,512]{2,1,0:T(8,128)S(1)} fusion(f32[8,60,512]{2,1,0:T(8,128)S(1)} %get-tuple-element.522, f32[8,60,512]{2,1,0:T(8,128)S(1)} %get-tuple-element.523, f32[8,60,512]{2,1,0:T(8,128)S(1)} %get-tuple-element.521, f32[8,60,512]{2,1,0:T(8,128)S(1)} %copy-done.24, f32[8,4,60,512]{3,2,1,0:T(8,128)} %convolution_bitcast_fusion.1, ...), kind=kOutput, calls=%fused_computation.110 | convolution fusion | flops 532807680 | bytes 6225920 | tf_op jit(solution)/shard_map/ij,sje->sie/dot_general | solution.py:61
  81.5 3.3 fusion.113
  85.3 3.7 fusion.107
  89.5 3.3 fusion.101
  93.2 3.3 fusion.95
  101.6 16.8 %all-gather.3 = f32[4,60,512]{2,1,0:T(8,128)} all-gather(f32[1,60,512]{2,1,0:T(8,128)S(1)} %bitcast.259), channel_id=2, replica_groups=mesh['sector'=8,'slab'=4] {'slab'}, dimensions={0}, use_global_device_ids=true | all-gather | bytes 614400 | tf_op jit(solution)/shard_map/all_gather | solution.py:35
  121.3 11.9 %while.91 = (s32[]{:T(128)}, f32[60,512]{1,0:T(8,128)}, f32[8,60,512]{2,1,0:T(8,128)S(1)}, f32[8,60,512]{2,1,0:T(8,128)S(1)}, s32[]{:T(128)}, /*index=5*/s32[]{:T(128)}) while((s32[]{:T(128)}, f32[60,512]{1,0:T(8,128)}, f32[8,60,512]{2,1,0:T(8,128)S(1)}, f32[8,60,512]{2,1,0:T(8,128)S(1)}, s32[]{:T(128)}, ...), condition=%wide.region_6.8_spmd.clone, body=%wide.region_5.7_spmd.clone.sunk | while | flops 92163 | bytes 491603 | solution.py:93
  137.0 15.4 %all-gather.4 = f32[4,60,512]{2,1,0:T(8,128)} all-gather(f32[1,60,512]{2,1,0:T(8,128)S(1)} %bitcast.260), channel_id=3, replica_groups=mesh['sector'=8,'slab'=4] {'slab'}, dimensions={0}, use_global_device_ids=true | all-gather | bytes 614400 | tf_op jit(solution)/shard_map/all_gather | solution.py:35
  153.1 2.9 while.92
  156.1 35.0 %all-reduce.6.cloned.1.call-done = (f32[60,512]{1,0:T(8,128)}, f32[60,512]{1,0:T(8,128)}) async-done(((f32[60,512]{1,0:T(8,128)}, f32[60,512]{1,0:T(8,128)}), (f32[60,512]{1,0:T(8,128)}, f32[60,512]{1,0:T(8,128)})) %all-reduce.6.cloned.1.call-update) | async-done | bytes 245776 | tf_op jit(solution)/shard_map/psum | solution.py:47
  193.6 12.8 %while.88 = (s32[]{:T(128)}, f32[60,512]{1,0:T(8,128)}, bf16[8,60,512]{2,1,0:T(8,128)(2,1)}, f32[8,60,512]{2,1,0:T(8,128)S(1)}, f32[8,60,512]{2,1,0:T(8,128)S(1)}, /*index=5*/s32[]{:T(128)}) while((s32[]{:T(128)}, f32[60,512]{1,0:T(8,128)}, bf16[8,60,512]{2,1,0:T(8,128)(2,1)}, f32[8,60,512]{2,1,0:T(8,128)S(1)}, ...), condition=%wide.region_11.13_spmd, body=%wide.region_10.12_spmd.sunk | while | flops 61442 | bytes 639557 | solution.py:107
  208.3 4.3 %convolution_bitcast_fusion = f32[8,4,60,512]{3,2,1,0:T(8,128)S(1)} fusion(f32[8,60,512]{2,1,0:T(8,128)S(1)} %multiply_add_fusion.1, f32[4,60,60]{2,0,1:T(4,128)S(1)} %copy-done.35), kind=kOutput, calls=%fused_computation.87 | convolution fusion | flops 707788800 | bytes 4972800 | tf_op jit(solution)/shard_map/dij,sje->sdie/dot_general | solution.py:53
  218.2 7.8 %collective-permute-done.3 = f32[8,60,192]{2,1,0:T(8,128)S(1)} collective-permute-done((f32[8,60,192]{2,1,0:T(8,128)S(1)}, f32[8,60,192]{2,1,0:T(8,128)S(1)}, u32[]{:S(2)}, u32[]{:S(2)}) %collective-permute-start.3) | collective-permute-done | bytes 368672 | tf_op jit(solution)/shard_map/ppermute | solution.py:24
  227.8 4.1 %copy.75 = f32[8,60,896]{1,0,2:T(8,128)} copy(f32[8,60,896]{2,1,0:T(8,128)} %pad_maximum_fusion) | data formatting | bytes 3440640 | tf_op jit(solution)/shard_map/concatenate | solution.py:22
  231.9 4.3 %gather_fusion.5 = f32[512,8,60]{2,1,0:T(8,128)} fusion(f32[8,60,896]{1,0,2:T(8,128)} %copy.75, s32[1024]{0:T(1024)S(1)} %copy-done.70), kind=kCustom, calls=%fused_computation.5.clone | custom fusion | bytes 1968128 | tf_op jit(solution)/shard_map/jit(_take)/gather | solution.py:57
  236.2 4.4 %gather_fusion.6 = f32[512,8,60]{2,1,0:T(8,128)} fusion(f32[8,60,896]{1,0,2:T(8,128)} %copy.75, s32[1024]{0:T(1024)S(1)} %copy-done.72), kind=kCustom, calls=%fused_computation.6.clone | custom fusion | bytes 1968128 | tf_op jit(solution)/shard_map/jit(_take)/gather | solution.py:57
  240.6 4.4 %gather_fusion.7 = f32[512,8,60]{2,1,0:T(8,128)} fusion(f32[8,60,896]{1,0,2:T(8,128)} %copy.75, s32[1024]{0:T(1024)S(1)} %copy-done.74), kind=kCustom, calls=%fused_computation.7.clone | custom fusion | bytes 1968128 | tf_op jit(solution)/shard_map/jit(_take)/gather | solution.py:57
  244.9 4.4 %gather_fusion.8 = f32[512,8,60]{2,1,0:T(8,128)} fusion(f32[8,60,896]{1,0,2:T(8,128)} %copy.75, s32[1024]{0:T(1024)S(1)} %copy-done.76), kind=kCustom, calls=%fused_computation.8.clone | custom fusion | bytes 1968128 | tf_op jit(solution)/shard_map/jit(_take)/gather | solution.py:57
  249.4 4.3 %gather_fusion.9 = f32[512,8,60]{2,1,0:T(8,128)} fusion(f32[8,60,896]{1,0,2:T(8,128)} %copy.75, s32[1024]{0:T(1024)S(1)} %copy-done.78), kind=kCustom, calls=%fused_computation.9.clone | custom fusion | bytes 1968128 | tf_op jit(solution)/shard_map/jit(_take)/gather | solution.py:57
  253.7 3.2 copy.76
  257.0 3.0 bitcast_multiply_fusion.18
  259.9 3.2 copy.78
  263.2 3.1 bitcast_multiply_fusion.15
  266.3 3.3 copy.80
  269.6 3.1 bitcast_multiply_fusion.12
  272.7 3.2 copy.82
  276.0 3.2 bitcast_multiply_fusion.9
  279.2 3.3 copy.84
  284.7 4.7 %fusion.89 = f32[8,60,512]{2,1,0:T(8,128)S(1)} fusion(f32[8,60,512]{2,1,0:T(8,128)S(1)} %copy-done.9, f32[8,60,512]{2,1,0:T(8,128)S(1)} %copy-done.10, f32[8,60,512]{2,1,0:T(8,128)S(1)} %get-tuple-element.506, f32[8,60,512]{2,1,0:T(8,128)S(1)} %copy-done.14, f32[8,4,60,512]{3,2,1,0:T(8,128)} %copy-done.4, f32[5,60,180]{2,1,0:T(8,128)S(1)} %copy-done.26), kind=kOutput, calls=%fused_computation.100 | convolution fusion | flops 532807680 | bytes 6225920 | tf_op jit(solution)/shard_map/ij,sje->sie/dot_general | solution.py:61
  289.4 3.6 fusion.83
  293.1 3.3 fusion.77
  296.5 4.1 %fusion.71 = f32[8,60,512]{2,1,0:T(8,128)S(1)} fusion(f32[8,60,512]{2,1,0:T(8,128)S(1)} %fusion.77, f32[8,60,512]{2,1,0:T(8,128)S(1)} %copy-done.22, f32[8,60,512]{2,1,0:T(8,128)S(1)} %copy-done.23, f32[8,60,512]{2,1,0:T(8,128)S(1)} %copy-done.21, f32[5,60,180]{2,1,0:T(8,128)} %param.39), kind=kOutput, calls=%fused_computation.94 | convolution fusion | flops 532561920 | bytes 4980736 | tf_op jit(solution)/shard_map/ij,sje->sie/dot_general | solution.py:61
  300.6 4.2 %fusion.65 = f32[8,60,512]{2,1,0:T(8,128)S(1)} fusion(f32[8,60,512]{2,1,0:T(8,128)S(1)} %fusion.71, f32[8,60,512]{2,1,0:T(8,128)S(1)} %get-tuple-element.495, f32[8,60,512]{2,1,0:T(8,128)S(1)} %get-tuple-element.496, f32[8,60,512]{2,1,0:T(8,128)S(1)} %get-tuple-element.494, f32[5,60,180]{2,1,0:T(8,128)} %param.39), kind=kOutput, calls=%fused_computation.92 | convolution fusion | flops 532561920 | bytes 4980736 | tf_op jit(solution)/shard_map/ij,sje->sie/dot_general | solution.py:61
  310.1 8.0 %while.93 = (s32[]{:T(128)}, f32[60,512]{1,0:T(8,128)S(1)}, f32[8,60,512]{2,1,0:T(8,128)S(1)}, f32[8,60,512]{2,1,0:T(8,128)}, s32[]{:T(128)}, /*index=5*/s32[]{:T(128)}) while((s32[]{:T(128)}, f32[60,512]{1,0:T(8,128)S(1)}, f32[8,60,512]{2,1,0:T(8,128)S(1)}, f32[8,60,512]{2,1,0:T(8,128)}, s32[]{:T(128)}, ...), condition=%wide.region_14.16_spmd.clone, body=%wide.region_13.15_spmd.clone.sunk | while | flops 92163 | bytes 491603 | solution.py:93
  318.2 16.2 %all-gather.5 = f32[4,60,512]{2,1,0:T(8,128)S(1)} all-gather(f32[1,60,512]{2,1,0:T(8,128)S(1)} %bitcast.261), channel_id=4, replica_groups=mesh['sector'=8,'slab'=4] {'slab'}, dimensions={0}, use_global_device_ids=true | all-gather | bytes 614400 | tf_op jit(solution)/shard_map/all_gather | solution.py:35
  338.2 34.2 %all-reduce.4.cloned.1.call-done = f32[60,512]{1,0:T(8,128)} async-done(((f32[60,512]{1,0:T(8,128)}), f32[60,512]{1,0:T(8,128)}) %all-reduce.4.cloned.1.call-update) | async-done | bytes 122896 | tf_op jit(solution)/shard_map/psum | solution.py:96
  373.4 8.2 %while.89 = (s32[]{:T(128)}, f32[60,512]{1,0:T(8,128)S(1)}, bf16[8,60,512]{2,1,0:T(8,128)(2,1)S(1)}, f32[8,60,512]{2,1,0:T(8,128)S(1)}, f32[8,60,512]{2,1,0:T(8,128)}, /*index=5*/s32[]{:T(128)}) while((s32[]{:T(128)}, f32[60,512]{1,0:T(8,128)S(1)}, bf16[8,60,512]{2,1,0:T(8,128)(2,1)S(1)}, f32[8,60,512]{2,1,0:T(8,128)S(1)}, ...), condition=%wide.region_19.21_spmd, body=%wide.region_18.20_spmd.sunk | while | flops 61442 | bytes 647241 | solution.py:107
  (306 shorter events, 110.1 us)
Async XLA Ops:
  7.2 89.4 %copy-start = (f32[60,60]{1,0:T(8,128)S(1)}, f32[60,60]{1,0:T(8,128)}, u32[]{:S(2)}) copy-start(f32[60,60]{1,0:T(8,128)} %param.40) | copy-start | bytes 43204
  7.2 15.4 %copy-start.3 = (f32[8,60,512]{2,0,1:T(8,128)S(1)}, f32[8,60,512]{2,0,1:T(8,128)}, u32[]{:S(2)}) copy-start(f32[8,60,512]{2,0,1:T(8,128)} %param.29) | copy-start | bytes 2949124
  7.2 10.6 %copy-start.79 = (s32[5,512]{1,0:T(8,128)S(1)}, s32[5,512]{1,0:T(8,128)}, u32[]{:S(2)}) copy-start(s32[5,512]{1,0:T(8,128)} %param.34) | copy-start | bytes 30724
  7.2 10.5 %copy-start.80 = (s32[5,512]{1,0:T(8,128)S(1)}, s32[5,512]{1,0:T(8,128)}, u32[]{:S(2)}) copy-start(s32[5,512]{1,0:T(8,128)} %param.35) | copy-start | bytes 30724
  7.2 13.9 %copy-start.81 = (s32[5,512]{1,0:T(8,128)S(1)}, s32[5,512]{1,0:T(8,128)}, u32[]{:S(2)}) copy-start(s32[5,512]{1,0:T(8,128)} %param.36) | copy-start | bytes 30724
  7.2 15.4 %copy-start.34 = (f32[4,60,60]{2,0,1:T(4,128)S(1)}, f32[4,60,60]{2,0,1:T(4,128)}, u32[]{:S(2)}) copy-start(f32[4,60,60]{2,0,1:T(4,128)} %param.38) | copy-start | bytes 172804
  9.6 23.1 %collective-permute-start = (f32[8,60,192]{2,0,1:T(8,128)}, f32[8,60,192]{2,0,1:T(8,128)S(1)}, u32[]{:S(2)}, u32[]{:S(2)}) collective-permute-start(f32[8,60,192]{2,0,1:T(8,128)} %get-tuple-element.526), channel_id=1, source_target_pairs={{0,4},{4,8},{8,12},{12,16},{16,20},{20,24},{24,28},{28,0},{1,5},{5... | collective-permute-start | bytes 1105928 | tf_op jit(solution)/shard_map/ppermute | solution.py:24
  10.0 22.6 %collective-permute-start.1 = (f32[8,60,192]{2,0,1:T(8,128)}, f32[8,60,192]{2,0,1:T(8,128)S(1)}, u32[]{:S(2)}, u32[]{:S(2)}) collective-permute-start(f32[8,60,192]{2,0,1:T(8,128)} %get-tuple-element.527), channel_id=1, source_target_pairs={{4,0},{8,4},{12,8},{16,12},{20,16},{24,20},{28,24},{0,28},{5,1},{9... | collective-permute-start | bytes 1105928 | tf_op jit(solution)/shard_map/ppermute | solution.py:26
  14.7 13.7 %copy-start.13 = (f32[8,60,512]{2,1,0:T(8,128)}, f32[8,60,512]{2,1,0:T(8,128)S(1)}, u32[]{:S(2)}) copy-start(f32[8,60,512]{2,1,0:T(8,128)S(1)} %copy.73) | copy-start | bytes 2949124
  15.4 81.2 %collective-permute-start.2 = (f32[60,512]{1,0:T(8,128)}, f32[60,512]{1,0:T(8,128)}, u32[]{:S(2)}, u32[]{:S(2)}) collective-permute-start(f32[60,512]{1,0:T(8,128)} %slice_bitcast_fusion.3), channel_id=1, source_target_pairs={{3,0},{0,1},{1,2},{2,3},{7,4},{4,5},{5,6},{6,7},{11,8},{8,9},{9,10... | collective-permute-start | bytes 368648 | tf_op jit(solution)/shard_map/ppermute | solution.py:14
  21.2 17.6 %copy-start.69 = (s32[1024]{0:T(1024)}, s32[1024]{0:T(1024)S(1)}, u32[]{:S(2)}) copy-start(s32[1024]{0:T(1024)S(1)} %pad_clamp_fusion.4) | copy-start | bytes 12292
  21.2 53.3 %copy-start.61 = (f32[1,512]{1,0:T(1,128)}, f32[1,512]{1,0:T(1,128)S(1)}, u32[]{:S(2)}) copy-start(f32[1,512]{1,0:T(1,128)S(1)} %get-tuple-element.545) | copy-start | bytes 6148
  21.2 59.8 %copy-start.55 = (f32[1,512]{1,0:T(1,128)}, f32[1,512]{1,0:T(1,128)S(1)}, u32[]{:S(2)}) copy-start(f32[1,512]{1,0:T(1,128)S(1)} %get-tuple-element.544) | copy-start | bytes 6148
  21.2 63.6 %copy-start.49 = (f32[1,512]{1,0:T(1,128)}, f32[1,512]{1,0:T(1,128)S(1)}, u32[]{:S(2)}) copy-start(f32[1,512]{1,0:T(1,128)S(1)} %get-tuple-element.543) | copy-start | bytes 6148
  21.2 67.8 %copy-start.43 = (f32[1,512]{1,0:T(1,128)}, f32[1,512]{1,0:T(1,128)S(1)}, u32[]{:S(2)}) copy-start(f32[1,512]{1,0:T(1,128)S(1)} %get-tuple-element.542) | copy-start | bytes 6148
  21.2 71.5 %copy-start.41 = (f32[1,512]{1,0:T(1,128)}, f32[1,512]{1,0:T(1,128)S(1)}, u32[]{:S(2)}) copy-start(f32[1,512]{1,0:T(1,128)S(1)} %get-tuple-element.541) | copy-start | bytes 6148
  21.3 25.1 %copy-start.71 = (s32[1024]{0:T(1024)}, s32[1024]{0:T(1024)S(1)}, u32[]{:S(2)}) copy-start(s32[1024]{0:T(1024)S(1)} %pad_clamp_fusion.3) | copy-start | bytes 12292
  21.3 32.6 %copy-start.73 = (s32[1024]{0:T(1024)}, s32[1024]{0:T(1024)S(1)}, u32[]{:S(2)}) copy-start(s32[1024]{0:T(1024)S(1)} %pad_clamp_fusion.2) | copy-start | bytes 12292
  21.3 40.1 %copy-start.75 = (s32[1024]{0:T(1024)}, s32[1024]{0:T(1024)S(1)}, u32[]{:S(2)}) copy-start(s32[1024]{0:T(1024)S(1)} %pad_clamp_fusion.1) | copy-start | bytes 12292
  22.6 58.4 %copy-start.63 = (f32[1,512]{1,0:T(1,128)}, f32[1,512]{1,0:T(1,128)S(1)}, u32[]{:S(2)}) copy-start(f32[1,512]{1,0:T(1,128)S(1)} %get-tuple-element.534) | copy-start | bytes 6148
  22.6 62.2 %copy-start.57 = (f32[1,512]{1,0:T(1,128)}, f32[1,512]{1,0:T(1,128)S(1)}, u32[]{:S(2)}) copy-start(f32[1,512]{1,0:T(1,128)S(1)} %get-tuple-element.533) | copy-start | bytes 6148
  22.6 62.2 %copy-start.59 = (f32[1,512]{1,0:T(1,128)}, f32[1,512]{1,0:T(1,128)S(1)}, u32[]{:S(2)}) copy-start(f32[1,512]{1,0:T(1,128)S(1)} %get-tuple-element.556) | copy-start | bytes 6148
  22.6 66.4 %copy-start.51 = (f32[1,512]{1,0:T(1,128)}, f32[1,512]{1,0:T(1,128)S(1)}, u32[]{:S(2)}) copy-start(f32[1,512]{1,0:T(1,128)S(1)} %get-tuple-element.532) | copy-start | bytes 6148
  22.6 66.4 %copy-start.53 = (f32[1,512]{1,0:T(1,128)}, f32[1,512]{1,0:T(1,128)S(1)}, u32[]{:S(2)}) copy-start(f32[1,512]{1,0:T(1,128)S(1)} %get-tuple-element.557) | copy-start | bytes 6148
  22.6 70.2 %copy-start.45 = (f32[1,512]{1,0:T(1,128)}, f32[1,512]{1,0:T(1,128)S(1)}, u32[]{:S(2)}) copy-start(f32[1,512]{1,0:T(1,128)S(1)} %get-tuple-element.531) | copy-start | bytes 6148
  22.6 70.2 %copy-start.47 = (f32[1,512]{1,0:T(1,128)}, f32[1,512]{1,0:T(1,128)S(1)}, u32[]{:S(2)}) copy-start(f32[1,512]{1,0:T(1,128)S(1)} %get-tuple-element.558) | copy-start | bytes 6148
  29.2 38.8 %copy-start.77 = (s32[1024]{0:T(1024)}, s32[1024]{0:T(1024)S(1)}, u32[]{:S(2)}) copy-start(s32[1024]{0:T(1024)S(1)} %pad_clamp_fusion) | copy-start | bytes 12292
  152.4 38.7 %all-reduce.6.cloned.1.call-start = ((), (), s32[]{:S(2)}) async-start(), calls=%async_computation.1 | async-start | bytes 524288 | tf_op jit(solution)/shard_map/psum | solution.py:47
  208.1 17.9 %copy-start.1 = (f32[8,60,512]{2,1,0:T(8,128)}, f32[8,60,512]{2,1,0:T(8,128)S(1)}, u32[]{:S(2)}) copy-start(f32[8,60,512]{2,1,0:T(8,128)S(1)} %multiply_add_fusion.1) | copy-start | bytes 2949124
  208.3 8.4 %copy-start.33 = (f32[8,3,512]{2,1,0:T(4,128)S(1)}, f32[8,3,512]{2,1,0:T(4,128)}, u32[]{:S(2)}) copy-start(f32[8,3,512]{2,1,0:T(4,128)} %copy-done.32) | copy-start | bytes 147460
  212.6 13.3 %collective-permute-start.3 = (f32[8,60,192]{2,1,0:T(8,128)S(1)}, f32[8,60,192]{2,1,0:T(8,128)S(1)}, u32[]{:S(2)}, u32[]{:S(2)}) collective-permute-start(f32[8,60,192]{2,1,0:T(8,128)S(1)} %get-tuple-element.524), channel_id=1, source_target_pairs={{0,4},{4,8},{8,12},{12,16},{16,20},{20,24},{24,28},{28,0},{1,5},{5... | collective-permute-start | bytes 1105928 | tf_op jit(solution)/shard_map/ppermute | solution.py:24
  212.7 13.3 %collective-permute-start.4 = (f32[8,60,192]{2,1,0:T(8,128)S(1)}, f32[8,60,192]{2,1,0:T(8,128)S(1)}, u32[]{:S(2)}, u32[]{:S(2)}) collective-permute-start(f32[8,60,192]{2,1,0:T(8,128)S(1)} %get-tuple-element.525), channel_id=1, source_target_pairs={{4,0},{8,4},{12,8},{16,12},{20,16},{24,20},{28,24},{0,28},{5,1},{9... | collective-permute-start | bytes 1105928 | tf_op jit(solution)/shard_map/ppermute | solution.py:26
  215.3 89.5 %collective-permute-start.5 = (f32[60,512]{1,0:T(8,128)S(1)}, f32[60,512]{1,0:T(8,128)}, u32[]{:S(2)}, u32[]{:S(2)}) collective-permute-start(f32[60,512]{1,0:T(8,128)S(1)} %slice_bitcast_fusion.2), channel_id=1, source_target_pairs={{3,0},{0,1},{1,2},{2,3},{7,4},{4,5},{5,6},{6,7},{11,8},{8,9},{9,10... | collective-permute-start | bytes 368648 | tf_op jit(solution)/shard_map/ppermute | solution.py:14
  227.7 8.4 %copy-start.72 = (s32[1024]{0:T(1024)S(1)}, s32[1024]{0:T(1024)}, u32[]{:S(2)}) copy-start(s32[1024]{0:T(1024)} %copy-done.71) | copy-start | bytes 12292
  231.9 8.7 %copy-start.74 = (s32[1024]{0:T(1024)S(1)}, s32[1024]{0:T(1024)}, u32[]{:S(2)}) copy-start(s32[1024]{0:T(1024)} %copy-done.73) | copy-start | bytes 12292
  231.9 13.0 %copy-start.76 = (s32[1024]{0:T(1024)S(1)}, s32[1024]{0:T(1024)}, u32[]{:S(2)}) copy-start(s32[1024]{0:T(1024)} %copy-done.75) | copy-start | bytes 12292
  236.2 13.2 %copy-start.78 = (s32[1024]{0:T(1024)S(1)}, s32[1024]{0:T(1024)}, u32[]{:S(2)}) copy-start(s32[1024]{0:T(1024)} %copy-done.77) | copy-start | bytes 12292
  249.4 7.6 %copy-start.62 = (f32[1,512]{1,0:T(1,128)S(1)}, f32[1,512]{1,0:T(1,128)}, u32[]{:S(2)}) copy-start(f32[1,512]{1,0:T(1,128)} %copy-done.61) | copy-start | bytes 6148
  249.4 7.6 %copy-start.67 = (f32[1,512]{1,0:T(1,128)S(1)}, f32[1,512]{1,0:T(1,128)}, u32[]{:S(2)}) copy-start(f32[1,512]{1,0:T(1,128)} %get-tuple-element.535) | copy-start | bytes 6148
  249.4 7.6 %copy-start.68 = (f32[1,512]{1,0:T(1,128)S(1)}, f32[1,512]{1,0:T(1,128)}, u32[]{:S(2)}) copy-start(f32[1,512]{1,0:T(1,128)} %get-tuple-element.554) | copy-start | bytes 6148
  249.4 7.6 %copy-start.90 = (pred[512]{0:T(512)(128)(4,1)S(1)}, pred[512]{0:T(512)(128)(4,1)}, u32[]{:S(2)}) copy-start(pred[512]{0:T(512)(128)(4,1)} %compare_and_fusion.4) | copy-start | bytes 1540
  275.9 6.6 %copy-start.42 = (f32[1,512]{1,0:T(1,128)S(1)}, f32[1,512]{1,0:T(1,128)}, u32[]{:S(2)}) copy-start(f32[1,512]{1,0:T(1,128)} %copy-done.41) | copy-start | bytes 6148
  275.9 6.5 %copy-start.46 = (f32[1,512]{1,0:T(1,128)S(1)}, f32[1,512]{1,0:T(1,128)}, u32[]{:S(2)}) copy-start(f32[1,512]{1,0:T(1,128)} %copy-done.45) | copy-start | bytes 6148
  307.6 10.6 %copy-start.5 = (f32[8,60,512]{2,1,0:T(8,128)}, f32[8,60,512]{2,1,0:T(8,128)S(1)}, u32[]{:S(2)}) copy-start(f32[8,60,512]{2,1,0:T(8,128)S(1)} %fusion.127) | copy-start | bytes 2949124
  307.6 10.6 %copy-start.28 = (f32[60,512]{1,0:T(8,128)S(1)}, f32[60,512]{1,0:T(8,128)}, u32[]{:S(2)}) copy-start(f32[60,512]{1,0:T(8,128)} %copy-done.27) | copy-start | bytes 368644
  318.2 16.2 %copy-start.31 = (f32[60,512]{1,0:T(8,128)}, f32[60,512]{1,0:T(8,128)S(1)}, u32[]{:S(2)}) copy-start(f32[60,512]{1,0:T(8,128)S(1)} %div.44) | copy-start | bytes 368644
  334.4 38.0 %all-reduce.4.cloned.1.call-start = ((), (), s32[]{:S(2)}) async-start(), calls=%async_computation | async-start | bytes 262144 | tf_op jit(solution)/shard_map/psum | solution.py:96
  335.3 46.3 %copy-start.2 = (f32[8,60,512]{2,1,0:T(8,128)S(1)}, f32[8,60,512]{2,1,0:T(8,128)}, u32[]{:S(2)}) copy-start(f32[8,60,512]{2,1,0:T(8,128)} %copy-done.1) | copy-start | bytes 2949124
  (54 other events, 230.9 us)
Sparse Core Ops, SparseCore 0:
  156.2 34.8 all-reduce.5
  338.2 34.1 all-reduce.3
where the time goes:
time: 397 us; the launch traced here: 391 us
  local copies, waits for them, and re-layouts  95.8 us (24%)
  other arithmetic  85.6 us (22%)
  waiting for transfers between devices  78.5 us (20%)
  matrix products  55.7 us (14%)
  blocking collectives  48.4 us (12%)
  between operations  16.7 us (4%)
  starting transfers between devices  9.72 us (2%)
    gather x20, local copies, waits for them, and re-layouts, operate(): picked = jnp.take(extended, place[face_id], axis=2)  73.6 us
    all_gather x3, blocking collectives, entering_2(): pieces = lax.all_gather(value, axis)  48.4 us
    dot_general x10, matrix products, operate(): jnp.einsum('ij,sje->sie', face_ops[face_id], stacked, precision=HIGH)  38.2 us
    psum x1, waiting for transfers between devices, broadcast(): return lax.psum(kept, axis)  35 us
    psum x1, waiting for transfers between devices, periodic_scan(): everything = lax.psum(scaled, 'slab')  34.2 us
    dynamic_update_slice x16, other arithmetic, periodic_scan(): _, solved = lax.scan(advance, entering, (factor, offset))  20.9 us
    add x16, other arithmetic, compose(): return (step_gain * state + step_offset, None)  19.8 us
    mul x10, other arithmetic, operate(): picked * masks[face_id, rotation][None, None, :]  17.5 us
  transfers between devices with their start and end apart: 8, of which 3 were waited for; matrix products, arithmetic and copies ran while one was open for 42% of the time, Pallas kernels for 0%

commit v1 on v0

--- a/solution.py
+++ b/solution.py
@@ -93,7 +93,11 @@
     own_offset, _ = lax.scan(compose, nothing, (factor, offset))
     scaled = own_offset / through_gain
     earlier = entering_2(scaled, "slab", adding_join, nothing)
-    everything = lax.psum(scaled, "slab")
+    everything = scaled
+    for hop_ in (1, 2):
+        everything = everything + lax.ppermute(
+            everything, "slab", [(dev, dev ^ hop_) for dev in range(4)]
+        )
     before_offset = before_gain * earlier
     total_offset = total_gain * everything
     closing = total_offset / (1.0 - total_gain)

time: 397 us -> 350 us (0.88)
  waiting for transfers between devices: 78.5 us -> 23.2 us
    psum x1 -> x0, waiting for transfers between devices: 34.2 us -> none  [periodic_scan(): everything = lax.psum(scaled, 'slab')]
    psum x1, waiting for transfers between devices: 35 us -> 11 us  [broadcast(): return lax.psum(kept, axis)]
    ppermute x0 -> x4, waiting for transfers between devices: none -> 4.5 us  [periodic_scan(): lax.ppermute(everything, 'slab', [(dev, dev ^ hop_) for dev in range(4)])]
    unnamed x188 -> x184, local copies, waits for them, and re-layouts: 8.84 us -> 8.18 us
  transfers between devices with their start and end apart: 8 -> 11, of which waited for: 3 -> 3; matrix products, arithmetic and copies ran while one was open for 42% -> 49% of each run, Pallas kernels for 0% -> 0%
where the time goes in v1:
time: 350 us; the launch traced here: 343 us
  local copies, waits for them, and re-layouts  95.1 us (27%)
  other arithmetic  87.7 us (25%)
  matrix products  55.7 us (16%)
  blocking collectives  51 us (15%)
  waiting for transfers between devices  23.2 us (7%)
  between operations  16.7 us (5%)
  starting transfers between devices  13.4 us (4%)
    gather x20, local copies, waits for them, and re-layouts, operate(): picked = jnp.take(extended, place[face_id], axis=2)  73.6 us
    all_gather x3, blocking collectives, entering_2(): pieces = lax.all_gather(value, axis)  51 us
    dot_general x10, matrix products, operate(): jnp.einsum('ij,sje->sie', face_ops[face_id], stacked, precision=HIGH)  38.2 us
    dynamic_update_slice x16, other arithmetic, periodic_scan(): _, solved = lax.scan(advance, entering, (factor, offset))  20.9 us
    add x16, other arithmetic, compose(): return (step_gain * state + step_offset, None)  19.8 us
    mul x10, other arithmetic, operate(): picked * masks[face_id, rotation][None, None, :]  17.5 us
    psum x1, waiting for transfers between devices, broadcast(): return lax.psum(kept, axis)  11 us
    dot_general x2, matrix products, operate(): terms = jnp.einsum('dij,sje->sdie', volume_ops, field, precision=HIGH)  9.45 us
  transfers between devices with their start and end apart: 11, of which 3 were waited for; matrix products, arithmetic and copies ran while one was open for 49% of the time, Pallas kernels for 0%

profile of v1, /device:TPU:0, one launch (start us, length us, event | category | flops | bytes accessed | tf_op | source)
XLA Modules:
  0.0 343.2 jit_solution(15913634291186957452)
XLA Ops:
  22.1 5.2 %convolution_bitcast_fusion.1 = f32[8,4,60,512]{3,2,1,0:T(8,128)} fusion(f32[8,60,512,1]{2,0,1,3:T(8,128)S(1)} %bitcast.258, f32[4,60,60]{2,0,1:T(4,128)S(1)} %copy-done.32), kind=kOutput, calls=%fused_computation.88 | convolution fusion | flops 707788800 | bytes 4972800 | tf_op jit(solution)/shard_map/dij,sje->sdie/dot_general | solution.py:53
  28.0 3.5 %fusion.1 = f32[8,60,512]{2,1,0:T(8,128)} fusion(f32[8,4,60,512]{3,2,1,0:T(8,128)} %convolution_bitcast_fusion.1, f32[8,3,512]{2,1,0:T(4,128)S(1)} %copy.59), kind=kLoop, calls=%fused_computation.26 | loop fusion | flops 1228800 | bytes 3981312 | tf_op jit(solution)/shard_map/reduce_sum | solution.py:54
  34.2 4.4 %copy.60 = f32[8,60,896]{1,0,2:T(8,128)} copy(f32[8,60,896]{2,0,1:T(8,128)} %pad_maximum_fusion.1) | data formatting | bytes 3440640 | tf_op jit(solution)/shard_map/concatenate | solution.py:22
  38.6 4.3 %gather_fusion = f32[512,8,60]{2,1,0:T(8,128)} fusion(f32[8,60,896]{1,0,2:T(8,128)} %copy.60, s32[1024]{0:T(1024)S(1)} %pad_clamp_fusion.4), kind=kCustom, calls=%fused_computation.clone | custom fusion | bytes 1968128 | tf_op jit(solution)/shard_map/jit(_take)/gather | solution.py:57
  43.0 3.2 copy.61
  46.2 4.3 %gather_fusion.1 = f32[512,8,60]{2,1,0:T(8,128)} fusion(f32[8,60,896]{1,0,2:T(8,128)} %copy.60, s32[1024]{0:T(1024)S(1)} %pad_clamp_fusion.3), kind=kCustom, calls=%fused_computation.1.clone | custom fusion | bytes 1968128 | tf_op jit(solution)/shard_map/jit(_take)/gather | solution.py:57
  50.5 3.2 copy.63
  53.7 4.3 %gather_fusion.2 = f32[512,8,60]{2,1,0:T(8,128)} fusion(f32[8,60,896]{1,0,2:T(8,128)} %copy.60, s32[1024]{0:T(1024)S(1)} %pad_clamp_fusion.2), kind=kCustom, calls=%fused_computation.2.clone | custom fusion | bytes 1968128 | tf_op jit(solution)/shard_map/jit(_take)/gather | solution.py:57
  58.0 3.2 copy.65
  61.2 4.3 %gather_fusion.3 = f32[512,8,60]{2,1,0:T(8,128)} fusion(f32[8,60,896]{1,0,2:T(8,128)} %copy.60, s32[1024]{0:T(1024)S(1)} %pad_clamp_fusion.1), kind=kCustom, calls=%fused_computation.3.clone | custom fusion | bytes 1968128 | tf_op jit(solution)/shard_map/jit(_take)/gather | solution.py:57
  67.8 4.3 %gather_fusion.4 = f32[512,8,60]{2,1,0:T(8,128)} fusion(f32[8,60,896]{1,0,2:T(8,128)} %copy.60, s32[1024]{0:T(1024)S(1)} %pad_clamp_fusion), kind=kCustom, calls=%fused_computation.4.clone | custom fusion | bytes 1968128 | tf_op jit(solution)/shard_map/jit(_take)/gather | solution.py:57
  76.2 4.6 %fusion.119 = f32[8,60,512]{2,1,0:T(8,128)S(1)} fusion(f32[8,60,512]{2,1,0:T(8,128)S(1)} %get-tuple-element.520, f32[8,60,512]{2,1,0:T(8,128)S(1)} %get-tuple-element.521, f32[8,60,512]{2,1,0:T(8,128)S(1)} %get-tuple-element.519, f32[8,60,512]{2,1,0:T(8,128)S(1)} %copy-done.24, f32[8,4,60,512]{3,2,1,0:T(8,128)} %convolution_bitcast_fusion.1, ...), kind=kOutput, calls=%fused_computation.110 | convolution fusion | flops 532807680 | bytes 6225920 | tf_op jit(solution)/shard_map/ij,sje->sie/dot_general | solution.py:61
  81.3 3.3 fusion.113
  85.1 3.7 %fusion.107 = f32[8,60,512]{2,1,0:T(8,128)S(1)} fusion(f32[8,60,512]{2,1,0:T(8,128)S(1)} %fusion.113, f32[8,60,512]{2,1,0:T(8,128)S(1)} %get-tuple-element.514, f32[8,60,512]{2,1,0:T(8,128)S(1)} %get-tuple-element.515, f32[8,60,512]{2,1,0:T(8,128)S(1)} %get-tuple-element.513, f32[5,60,180]{2,1,0:T(8,128)S(1)} %copy-done.25), kind=kOutput, calls=%fused_computation.106 | convolution fusion | flops 532561920 | bytes 5242880 | tf_op jit(solution)/shard_map/ij,sje->sie/dot_general | solution.py:61
  89.3 3.3 fusion.101
  93.1 3.3 fusion.95
  101.4 16.8 %all-gather.3 = f32[4,60,512]{2,1,0:T(8,128)} all-gather(f32[1,60,512]{2,1,0:T(8,128)S(1)} %bitcast.259), channel_id=2, replica_groups=mesh['sector'=8,'slab'=4] {'slab'}, dimensions={0}, use_global_device_ids=true | all-gather | bytes 614400 | tf_op jit(solution)/shard_map/all_gather | solution.py:35
  121.1 11.9 %while.91 = (s32[]{:T(128)}, f32[60,512]{1,0:T(8,128)}, f32[8,60,512]{2,1,0:T(8,128)S(1)}, f32[8,60,512]{2,1,0:T(8,128)S(1)}, s32[]{:T(128)}, /*index=5*/s32[]{:T(128)}) while((s32[]{:T(128)}, f32[60,512]{1,0:T(8,128)}, f32[8,60,512]{2,1,0:T(8,128)S(1)}, f32[8,60,512]{2,1,0:T(8,128)S(1)}, s32[]{:T(128)}, ...), condition=%wide.region_6.8_spmd.clone, body=%wide.region_5.7_spmd.clone.sunk | while | flops 92163 | bytes 491603 | solution.py:93
  136.8 17.9 %all-gather.4 = f32[4,60,512]{2,1,0:T(8,128)} all-gather(f32[1,60,512]{2,1,0:T(8,128)} %bitcast.58), channel_id=3, replica_groups=mesh['sector'=8,'slab'=4] {'slab'}, dimensions={0}, use_global_device_ids=true | all-gather | bytes 614400 | tf_op jit(solution)/shard_map/all_gather | solution.py:35
  157.7 2.9 while.92
  160.6 11.0 %all-reduce.2.cloned.1.call-done = f32[60,512]{1,0:T(8,128)} async-done(((f32[60,512]{1,0:T(8,128)}), f32[60,512]{1,0:T(8,128)}) %all-reduce.2.cloned.1.call-update) | async-done | bytes 122896 | tf_op jit(solution)/shard_map/psum | solution.py:47
  174.2 12.8 %while.88 = (s32[]{:T(128)}, f32[60,512]{1,0:T(8,128)}, bf16[8,60,512]{2,1,0:T(8,128)(2,1)}, f32[8,60,512]{2,1,0:T(8,128)S(1)}, f32[8,60,512]{2,1,0:T(8,128)S(1)}, /*index=5*/s32[]{:T(128)}) while((s32[]{:T(128)}, f32[60,512]{1,0:T(8,128)}, bf16[8,60,512]{2,1,0:T(8,128)(2,1)}, f32[8,60,512]{2,1,0:T(8,128)S(1)}, ...), condition=%wide.region_10.12_spmd, body=%wide.region_9.11_spmd.sunk | while | flops 61442 | bytes 639557 | solution.py:111
  188.9 4.3 %convolution_bitcast_fusion = f32[8,4,60,512]{3,2,1,0:T(8,128)S(1)} fusion(f32[8,60,512]{2,1,0:T(8,128)S(1)} %multiply_add_fusion.1, f32[4,60,60]{2,0,1:T(4,128)S(1)} %copy-done.33), kind=kOutput, calls=%fused_computation.87 | convolution fusion | flops 707788800 | bytes 4972800 | tf_op jit(solution)/shard_map/dij,sje->sdie/dot_general | solution.py:53
  198.9 7.6 %collective-permute-done.5 = f32[8,60,192]{2,1,0:T(8,128)S(1)} collective-permute-done((f32[8,60,192]{2,1,0:T(8,128)S(1)}, f32[8,60,192]{2,1,0:T(8,128)S(1)}, u32[]{:S(2)}, u32[]{:S(2)}) %collective-permute-start.5) | collective-permute-done | bytes 368672 | tf_op jit(solution)/shard_map/ppermute | solution.py:24
  208.3 4.1 %copy.75 = f32[8,60,896]{1,0,2:T(8,128)} copy(f32[8,60,896]{2,1,0:T(8,128)} %pad_maximum_fusion) | data formatting | bytes 3440640 | tf_op jit(solution)/shard_map/concatenate | solution.py:22
  212.4 4.3 %gather_fusion.5 = f32[512,8,60]{2,1,0:T(8,128)} fusion(f32[8,60,896]{1,0,2:T(8,128)} %copy.75, s32[1024]{0:T(1024)S(1)} %copy-done.68), kind=kCustom, calls=%fused_computation.5.clone | custom fusion | bytes 1968128 | tf_op jit(solution)/shard_map/jit(_take)/gather | solution.py:57
  216.8 4.4 %gather_fusion.6 = f32[512,8,60]{2,1,0:T(8,128)} fusion(f32[8,60,896]{1,0,2:T(8,128)} %copy.75, s32[1024]{0:T(1024)S(1)} %copy-done.70), kind=kCustom, calls=%fused_computation.6.clone | custom fusion | bytes 1968128 | tf_op jit(solution)/shard_map/jit(_take)/gather | solution.py:57
  221.1 4.4 %gather_fusion.7 = f32[512,8,60]{2,1,0:T(8,128)} fusion(f32[8,60,896]{1,0,2:T(8,128)} %copy.75, s32[1024]{0:T(1024)S(1)} %copy-done.72), kind=kCustom, calls=%fused_computation.7.clone | custom fusion | bytes 1968128 | tf_op jit(solution)/shard_map/jit(_take)/gather | solution.py:57
  225.5 4.4 %gather_fusion.8 = f32[512,8,60]{2,1,0:T(8,128)} fusion(f32[8,60,896]{1,0,2:T(8,128)} %copy.75, s32[1024]{0:T(1024)S(1)} %copy-done.74), kind=kCustom, calls=%fused_computation.8.clone | custom fusion | bytes 1968128 | tf_op jit(solution)/shard_map/jit(_take)/gather | solution.py:57
  229.9 4.3 %gather_fusion.9 = f32[512,8,60]{2,1,0:T(8,128)} fusion(f32[8,60,896]{1,0,2:T(8,128)} %copy.75, s32[1024]{0:T(1024)S(1)} %copy-done.76), kind=kCustom, calls=%fused_computation.9.clone | custom fusion | bytes 1968128 | tf_op jit(solution)/shard_map/jit(_take)/gather | solution.py:57
  234.3 3.2 copy.76
  237.5 3.0 bitcast_multiply_fusion.18
  240.5 3.2 copy.78
  243.8 3.1 bitcast_multiply_fusion.15
  246.8 3.3 copy.80
  250.1 3.1 bitcast_multiply_fusion.12
  253.3 3.2 copy.82
  256.5 3.2 bitcast_multiply_fusion.9
  259.7 3.3 copy.84
  265.2 4.7 %fusion.89 = f32[8,60,512]{2,1,0:T(8,128)S(1)} fusion(f32[8,60,512]{2,1,0:T(8,128)S(1)} %copy-done.9, f32[8,60,512]{2,1,0:T(8,128)S(1)} %copy-done.10, f32[8,60,512]{2,1,0:T(8,128)S(1)} %get-tuple-element.504, f32[8,60,512]{2,1,0:T(8,128)S(1)} %copy-done.14, f32[8,4,60,512]{3,2,1,0:T(8,128)} %copy-done.4, f32[5,60,180]{2,1,0:T(8,128)S(1)} %copy-done.26), kind=kOutput, calls=%fused_computation.100 | convolution fusion | flops 532807680 | bytes 6225920 | tf_op jit(solution)/shard_map/ij,sje->sie/dot_general | solution.py:61
  270.0 3.6 %fusion.83 = f32[8,60,512]{2,1,0:T(8,128)S(1)} fusion(f32[8,60,512]{2,1,0:T(8,128)S(1)} %fusion.89, f32[8,60,512]{2,1,0:T(8,128)S(1)} %copy-done.16, f32[8,60,512]{2,1,0:T(8,128)S(1)} %copy-done.17, f32[8,60,512]{2,1,0:T(8,128)S(1)} %copy-done.15, f32[5,60,180]{2,1,0:T(8,128)S(1)} %copy-done.26), kind=kOutput, calls=%fused_computation.98 | convolution fusion | flops 532561920 | bytes 5242880 | tf_op jit(solution)/shard_map/ij,sje->sie/dot_general | solution.py:61
  273.7 3.3 fusion.77
  277.0 4.1 %fusion.71 = f32[8,60,512]{2,1,0:T(8,128)S(1)} fusion(f32[8,60,512]{2,1,0:T(8,128)S(1)} %fusion.77, f32[8,60,512]{2,1,0:T(8,128)S(1)} %copy-done.22, f32[8,60,512]{2,1,0:T(8,128)S(1)} %copy-done.23, f32[8,60,512]{2,1,0:T(8,128)S(1)} %copy-done.21, f32[5,60,180]{2,1,0:T(8,128)} %param.39), kind=kOutput, calls=%fused_computation.94 | convolution fusion | flops 532561920 | bytes 4980736 | tf_op jit(solution)/shard_map/ij,sje->sie/dot_general | solution.py:61
  281.2 4.2 %fusion.65 = f32[8,60,512]{2,1,0:T(8,128)S(1)} fusion(f32[8,60,512]{2,1,0:T(8,128)S(1)} %fusion.71, f32[8,60,512]{2,1,0:T(8,128)S(1)} %get-tuple-element.493, f32[8,60,512]{2,1,0:T(8,128)S(1)} %get-tuple-element.494, f32[8,60,512]{2,1,0:T(8,128)S(1)} %get-tuple-element.492, f32[5,60,180]{2,1,0:T(8,128)} %param.39), kind=kOutput, calls=%fused_computation.92 | convolution fusion | flops 532561920 | bytes 4980736 | tf_op jit(solution)/shard_map/ij,sje->sie/dot_general | solution.py:61
  290.7 8.0 %while.93 = (s32[]{:T(128)}, f32[60,512]{1,0:T(8,128)S(1)}, f32[8,60,512]{2,1,0:T(8,128)S(1)}, f32[8,60,512]{2,1,0:T(8,128)}, s32[]{:T(128)}, /*index=5*/s32[]{:T(128)}) while((s32[]{:T(128)}, f32[60,512]{1,0:T(8,128)S(1)}, f32[8,60,512]{2,1,0:T(8,128)S(1)}, f32[8,60,512]{2,1,0:T(8,128)}, s32[]{:T(128)}, ...), condition=%wide.region_13.15_spmd.clone, body=%wide.region_12.14_spmd.clone.sunk | while | flops 92163 | bytes 491603 | solution.py:93
  300.3 16.3 %all-gather.5 = f32[4,60,512]{2,1,0:T(8,128)S(1)} all-gather(f32[1,60,512]{2,1,0:T(8,128)S(1)} %bitcast.260), channel_id=4, replica_groups=mesh['sector'=8,'slab'=4] {'slab'}, dimensions={0}, use_global_device_ids=true | all-gather | bytes 614400 | tf_op jit(solution)/shard_map/all_gather | solution.py:35
  320.5 4.5 %collective-permute-done.9 = f32[60,512]{1,0:T(8,128)S(1)} collective-permute-done((f32[60,512]{1,0:T(8,128)S(1)}, f32[60,512]{1,0:T(8,128)S(1)}, u32[]{:S(2)}, u32[]{:S(2)}) %collective-permute-start.9) | collective-permute-done | bytes 122912 | tf_op jit(solution)/shard_map/ppermute | solution.py:98
  326.0 8.2 %while.89 = (s32[]{:T(128)}, f32[60,512]{1,0:T(8,128)S(1)}, bf16[8,60,512]{2,1,0:T(8,128)(2,1)S(1)}, f32[8,60,512]{2,1,0:T(8,128)S(1)}, f32[8,60,512]{2,1,0:T(8,128)}, /*index=5*/s32[]{:T(128)}) while((s32[]{:T(128)}, f32[60,512]{1,0:T(8,128)S(1)}, bf16[8,60,512]{2,1,0:T(8,128)(2,1)S(1)}, f32[8,60,512]{2,1,0:T(8,128)S(1)}, ...), condition=%wide.region_17.19_spmd, body=%wide.region_16.18_spmd.sunk | while | flops 61442 | bytes 647241 | solution.py:111
  (309 shorter events, 113.9 us)
Async XLA Ops:
  7.2 89.3 %copy-start = (f32[60,60]{1,0:T(8,128)S(1)}, f32[60,60]{1,0:T(8,128)}, u32[]{:S(2)}) copy-start(f32[60,60]{1,0:T(8,128)} %param.40) | copy-start | bytes 43204
  7.2 14.9 %copy-start.3 = (f32[8,60,512]{2,0,1:T(8,128)S(1)}, f32[8,60,512]{2,0,1:T(8,128)}, u32[]{:S(2)}) copy-start(f32[8,60,512]{2,0,1:T(8,128)} %param.29) | copy-start | bytes 2949124
  7.2 10.6 %copy-start.77 = (s32[5,512]{1,0:T(8,128)S(1)}, s32[5,512]{1,0:T(8,128)}, u32[]{:S(2)}) copy-start(s32[5,512]{1,0:T(8,128)} %param.34) | copy-start | bytes 30724
  7.2 10.6 %copy-start.78 = (s32[5,512]{1,0:T(8,128)S(1)}, s32[5,512]{1,0:T(8,128)}, u32[]{:S(2)}) copy-start(s32[5,512]{1,0:T(8,128)} %param.35) | copy-start | bytes 30724
  7.2 13.4 %copy-start.79 = (s32[5,512]{1,0:T(8,128)S(1)}, s32[5,512]{1,0:T(8,128)}, u32[]{:S(2)}) copy-start(s32[5,512]{1,0:T(8,128)} %param.36) | copy-start | bytes 30724
  7.2 14.9 %copy-start.32 = (f32[4,60,60]{2,0,1:T(4,128)S(1)}, f32[4,60,60]{2,0,1:T(4,128)}, u32[]{:S(2)}) copy-start(f32[4,60,60]{2,0,1:T(4,128)} %param.38) | copy-start | bytes 172804
  7.2 164.4 %all-reduce.2.cloned.1.call-start = ((), (), s32[]{:S(2)}) async-start(), calls=%async_computation | async-start | bytes 262144 | tf_op jit(solution)/shard_map/psum | solution.py:47
  9.6 21.8 %collective-permute-start = (f32[8,60,192]{2,0,1:T(8,128)}, f32[8,60,192]{2,0,1:T(8,128)S(1)}, u32[]{:S(2)}, u32[]{:S(2)}) collective-permute-start(f32[8,60,192]{2,0,1:T(8,128)} %get-tuple-element.524), channel_id=1, source_target_pairs={{0,4},{4,8},{8,12},{12,16},{16,20},{20,24},{24,28},{28,0},{1,5},{5... | collective-permute-start | bytes 1105928 | tf_op jit(solution)/shard_map/ppermute | solution.py:24
  10.1 21.4 %collective-permute-start.1 = (f32[8,60,192]{2,0,1:T(8,128)}, f32[8,60,192]{2,0,1:T(8,128)}, u32[]{:S(2)}, u32[]{:S(2)}) collective-permute-start(f32[8,60,192]{2,0,1:T(8,128)} %get-tuple-element.525), channel_id=1, source_target_pairs={{4,0},{8,4},{12,8},{16,12},{20,16},{24,20},{28,24},{0,28},{5,1},{9... | collective-permute-start | bytes 1105928 | tf_op jit(solution)/shard_map/ppermute | solution.py:26
  14.7 13.1 %copy-start.13 = (f32[8,60,512]{2,1,0:T(8,128)}, f32[8,60,512]{2,1,0:T(8,128)S(1)}, u32[]{:S(2)}) copy-start(f32[8,60,512]{2,1,0:T(8,128)S(1)} %copy.73) | copy-start | bytes 2949124
  15.5 81.0 %collective-permute-start.2 = (f32[60,512]{1,0:T(8,128)}, f32[60,512]{1,0:T(8,128)}, u32[]{:S(2)}, u32[]{:S(2)}) collective-permute-start(f32[60,512]{1,0:T(8,128)} %slice_bitcast_fusion.3), channel_id=1, source_target_pairs={{3,0},{0,1},{1,2},{2,3},{7,4},{4,5},{5,6},{6,7},{11,8},{8,9},{9,10... | collective-permute-start | bytes 368648 | tf_op jit(solution)/shard_map/ppermute | solution.py:14
  20.6 18.0 %copy-start.67 = (s32[1024]{0:T(1024)}, s32[1024]{0:T(1024)S(1)}, u32[]{:S(2)}) copy-start(s32[1024]{0:T(1024)S(1)} %pad_clamp_fusion.4) | copy-start | bytes 12292
  20.7 53.7 %copy-start.59 = (f32[1,512]{1,0:T(1,128)}, f32[1,512]{1,0:T(1,128)S(1)}, u32[]{:S(2)}) copy-start(f32[1,512]{1,0:T(1,128)S(1)} %get-tuple-element.543) | copy-start | bytes 6148
  20.7 60.1 %copy-start.53 = (f32[1,512]{1,0:T(1,128)}, f32[1,512]{1,0:T(1,128)S(1)}, u32[]{:S(2)}) copy-start(f32[1,512]{1,0:T(1,128)S(1)} %get-tuple-element.542) | copy-start | bytes 6148
  20.7 64.0 %copy-start.47 = (f32[1,512]{1,0:T(1,128)}, f32[1,512]{1,0:T(1,128)S(1)}, u32[]{:S(2)}) copy-start(f32[1,512]{1,0:T(1,128)S(1)} %get-tuple-element.541) | copy-start | bytes 6148
  20.7 68.2 %copy-start.41 = (f32[1,512]{1,0:T(1,128)}, f32[1,512]{1,0:T(1,128)S(1)}, u32[]{:S(2)}) copy-start(f32[1,512]{1,0:T(1,128)S(1)} %get-tuple-element.540) | copy-start | bytes 6148
  20.7 71.9 %copy-start.39 = (f32[1,512]{1,0:T(1,128)}, f32[1,512]{1,0:T(1,128)S(1)}, u32[]{:S(2)}) copy-start(f32[1,512]{1,0:T(1,128)S(1)} %get-tuple-element.539) | copy-start | bytes 6148
  20.7 25.4 %copy-start.69 = (s32[1024]{0:T(1024)}, s32[1024]{0:T(1024)S(1)}, u32[]{:S(2)}) copy-start(s32[1024]{0:T(1024)S(1)} %pad_clamp_fusion.3) | copy-start | bytes 12292
  20.8 33.0 %copy-start.71 = (s32[1024]{0:T(1024)}, s32[1024]{0:T(1024)S(1)}, u32[]{:S(2)}) copy-start(s32[1024]{0:T(1024)S(1)} %pad_clamp_fusion.2) | copy-start | bytes 12292
  20.8 40.5 %copy-start.73 = (s32[1024]{0:T(1024)}, s32[1024]{0:T(1024)S(1)}, u32[]{:S(2)}) copy-start(s32[1024]{0:T(1024)S(1)} %pad_clamp_fusion.1) | copy-start | bytes 12292
  22.0 58.8 %copy-start.61 = (f32[1,512]{1,0:T(1,128)}, f32[1,512]{1,0:T(1,128)S(1)}, u32[]{:S(2)}) copy-start(f32[1,512]{1,0:T(1,128)S(1)} %get-tuple-element.532) | copy-start | bytes 6148
  22.1 62.6 %copy-start.55 = (f32[1,512]{1,0:T(1,128)}, f32[1,512]{1,0:T(1,128)S(1)}, u32[]{:S(2)}) copy-start(f32[1,512]{1,0:T(1,128)S(1)} %get-tuple-element.531) | copy-start | bytes 6148
  22.1 62.6 %copy-start.57 = (f32[1,512]{1,0:T(1,128)}, f32[1,512]{1,0:T(1,128)S(1)}, u32[]{:S(2)}) copy-start(f32[1,512]{1,0:T(1,128)S(1)} %get-tuple-element.554) | copy-start | bytes 6148
  22.1 66.8 %copy-start.49 = (f32[1,512]{1,0:T(1,128)}, f32[1,512]{1,0:T(1,128)S(1)}, u32[]{:S(2)}) copy-start(f32[1,512]{1,0:T(1,128)S(1)} %get-tuple-element.530) | copy-start | bytes 6148
  22.1 66.8 %copy-start.51 = (f32[1,512]{1,0:T(1,128)}, f32[1,512]{1,0:T(1,128)S(1)}, u32[]{:S(2)}) copy-start(f32[1,512]{1,0:T(1,128)S(1)} %get-tuple-element.555) | copy-start | bytes 6148
  22.1 70.6 %copy-start.43 = (f32[1,512]{1,0:T(1,128)}, f32[1,512]{1,0:T(1,128)S(1)}, u32[]{:S(2)}) copy-start(f32[1,512]{1,0:T(1,128)S(1)} %get-tuple-element.529) | copy-start | bytes 6148
  22.1 70.6 %copy-start.45 = (f32[1,512]{1,0:T(1,128)}, f32[1,512]{1,0:T(1,128)S(1)}, u32[]{:S(2)}) copy-start(f32[1,512]{1,0:T(1,128)S(1)} %get-tuple-element.556) | copy-start | bytes 6148
  28.0 39.8 %copy-start.75 = (s32[1024]{0:T(1024)}, s32[1024]{0:T(1024)S(1)}, u32[]{:S(2)}) copy-start(s32[1024]{0:T(1024)S(1)} %pad_clamp_fusion) | copy-start | bytes 12292
  136.8 18.0 %collective-permute-start.3 = (f32[60,512]{1,0:T(8,128)}, f32[60,512]{1,0:T(8,128)}, u32[]{:S(2)}, u32[]{:S(2)}) collective-permute-start(f32[60,512]{1,0:T(8,128)} %div.41), channel_id=1, source_target_pairs={{0,1},{1,0},{2,3},{3,2},{4,5},{5,4},{6,7},{7,6},{8,9},{9,8},{10,11... | collective-permute-start | bytes 368648 | tf_op jit(solution)/shard_map/ppermute | solution.py:98
  156.4 15.2 %collective-permute-start.4 = (f32[60,512]{1,0:T(8,128)}, f32[60,512]{1,0:T(8,128)}, u32[]{:S(2)}, u32[]{:S(2)}) collective-permute-start(f32[60,512]{1,0:T(8,128)} %add.194), channel_id=1, source_target_pairs={{0,2},{1,3},{2,0},{3,1},{4,6},{5,7},{6,4},{7,5},{8,10},{9,11},{10,... | collective-permute-start | bytes 368648 | tf_op jit(solution)/shard_map/ppermute | solution.py:98
  188.7 17.8 %copy-start.1 = (f32[8,60,512]{2,1,0:T(8,128)}, f32[8,60,512]{2,1,0:T(8,128)S(1)}, u32[]{:S(2)}) copy-start(f32[8,60,512]{2,1,0:T(8,128)S(1)} %multiply_add_fusion.1) | copy-start | bytes 2949124
  188.9 8.5 %copy-start.31 = (f32[8,3,512]{2,1,0:T(4,128)S(1)}, f32[8,3,512]{2,1,0:T(4,128)}, u32[]{:S(2)}) copy-start(f32[8,3,512]{2,1,0:T(4,128)} %copy-done.30) | copy-start | bytes 147460
  193.2 13.3 %collective-permute-start.5 = (f32[8,60,192]{2,1,0:T(8,128)S(1)}, f32[8,60,192]{2,1,0:T(8,128)S(1)}, u32[]{:S(2)}, u32[]{:S(2)}) collective-permute-start(f32[8,60,192]{2,1,0:T(8,128)S(1)} %get-tuple-element.522), channel_id=1, source_target_pairs={{0,4},{4,8},{8,12},{12,16},{16,20},{20,24},{24,28},{28,0},{1,5},{5... | collective-permute-start | bytes 1105928 | tf_op jit(solution)/shard_map/ppermute | solution.py:24
  193.3 13.2 %collective-permute-start.6 = (f32[8,60,192]{2,1,0:T(8,128)S(1)}, f32[8,60,192]{2,1,0:T(8,128)S(1)}, u32[]{:S(2)}, u32[]{:S(2)}) collective-permute-start(f32[8,60,192]{2,1,0:T(8,128)S(1)} %get-tuple-element.523), channel_id=1, source_target_pairs={{4,0},{8,4},{12,8},{16,12},{20,16},{24,20},{28,24},{0,28},{5,1},{9... | collective-permute-start | bytes 1105928 | tf_op jit(solution)/shard_map/ppermute | solution.py:26
  195.9 89.4 %collective-permute-start.7 = (f32[60,512]{1,0:T(8,128)S(1)}, f32[60,512]{1,0:T(8,128)}, u32[]{:S(2)}, u32[]{:S(2)}) collective-permute-start(f32[60,512]{1,0:T(8,128)S(1)} %slice_bitcast_fusion.2), channel_id=1, source_target_pairs={{3,0},{0,1},{1,2},{2,3},{7,4},{4,5},{5,6},{6,7},{11,8},{8,9},{9,10... | collective-permute-start | bytes 368648 | tf_op jit(solution)/shard_map/ppermute | solution.py:14
  208.3 8.4 %copy-start.70 = (s32[1024]{0:T(1024)S(1)}, s32[1024]{0:T(1024)}, u32[]{:S(2)}) copy-start(s32[1024]{0:T(1024)} %copy-done.69) | copy-start | bytes 12292
  212.4 8.7 %copy-start.72 = (s32[1024]{0:T(1024)S(1)}, s32[1024]{0:T(1024)}, u32[]{:S(2)}) copy-start(s32[1024]{0:T(1024)} %copy-done.71) | copy-start | bytes 12292
  212.4 13.0 %copy-start.74 = (s32[1024]{0:T(1024)S(1)}, s32[1024]{0:T(1024)}, u32[]{:S(2)}) copy-start(s32[1024]{0:T(1024)} %copy-done.73) | copy-start | bytes 12292
  216.8 13.2 %copy-start.76 = (s32[1024]{0:T(1024)S(1)}, s32[1024]{0:T(1024)}, u32[]{:S(2)}) copy-start(s32[1024]{0:T(1024)} %copy-done.75) | copy-start | bytes 12292
  229.9 7.6 %copy-start.60 = (f32[1,512]{1,0:T(1,128)S(1)}, f32[1,512]{1,0:T(1,128)}, u32[]{:S(2)}) copy-start(f32[1,512]{1,0:T(1,128)} %copy-done.59) | copy-start | bytes 6148
  229.9 7.6 %copy-start.65 = (f32[1,512]{1,0:T(1,128)S(1)}, f32[1,512]{1,0:T(1,128)}, u32[]{:S(2)}) copy-start(f32[1,512]{1,0:T(1,128)} %get-tuple-element.533) | copy-start | bytes 6148
  229.9 7.6 %copy-start.66 = (f32[1,512]{1,0:T(1,128)S(1)}, f32[1,512]{1,0:T(1,128)}, u32[]{:S(2)}) copy-start(f32[1,512]{1,0:T(1,128)} %get-tuple-element.552) | copy-start | bytes 6148
  229.9 7.6 %copy-start.88 = (pred[512]{0:T(512)(128)(4,1)S(1)}, pred[512]{0:T(512)(128)(4,1)}, u32[]{:S(2)}) copy-start(pred[512]{0:T(512)(128)(4,1)} %compare_and_fusion.4) | copy-start | bytes 1540
  288.1 10.6 %copy-start.5 = (f32[8,60,512]{2,1,0:T(8,128)}, f32[8,60,512]{2,1,0:T(8,128)S(1)}, u32[]{:S(2)}) copy-start(f32[8,60,512]{2,1,0:T(8,128)S(1)} %fusion.127) | copy-start | bytes 2949124
  288.1 10.6 %copy-start.28 = (f32[60,512]{1,0:T(8,128)S(1)}, f32[60,512]{1,0:T(8,128)}, u32[]{:S(2)}) copy-start(f32[60,512]{1,0:T(8,128)} %copy-done.27) | copy-start | bytes 368644
  298.8 17.8 %collective-permute-start.8 = (f32[60,512]{1,0:T(8,128)S(1)}, f32[60,512]{1,0:T(8,128)S(1)}, u32[]{:S(2)}, u32[]{:S(2)}) collective-permute-start(f32[60,512]{1,0:T(8,128)S(1)} %div.44), channel_id=1, source_target_pairs={{0,1},{1,0},{2,3},{3,2},{4,5},{5,4},{6,7},{7,6},{8,9},{9,8},{10,11... | collective-permute-start | bytes 368648 | tf_op jit(solution)/shard_map/ppermute | solution.py:98
  316.6 8.3 %collective-permute-start.9 = (f32[60,512]{1,0:T(8,128)S(1)}, f32[60,512]{1,0:T(8,128)S(1)}, u32[]{:S(2)}, u32[]{:S(2)}) collective-permute-start(f32[60,512]{1,0:T(8,128)S(1)} %add.204), channel_id=1, source_target_pairs={{0,2},{1,3},{2,0},{3,1},{4,6},{5,7},{6,4},{7,5},{8,10},{9,11},{10,... | collective-permute-start | bytes 368648 | tf_op jit(solution)/shard_map/ppermute | solution.py:98
  317.6 16.5 %copy-start.2 = (f32[8,60,512]{2,1,0:T(8,128)S(1)}, f32[8,60,512]{2,1,0:T(8,128)}, u32[]{:S(2)}) copy-start(f32[8,60,512]{2,1,0:T(8,128)} %copy-done.1) | copy-start | bytes 2949124
  (55 other events, 243.9 us)
Sparse Core Ops, SparseCore 0:
  137.0 34.5 all-reduce.1
